TPU v7x, 256 devices: a whole 4x4x8 slice. The times are simulated.
256 devices in a mesh: gx: 32 (over y, z), gy: 8 (over x, core).
Axes of the slice: x: 4, y: 4, z: 8, core: 2. Of those that a mesh axis runs over, the one named last changes fastest.
Arguments:
- offsets: float32 [3, 64, 16, 1024], P(None, 'gx', 'gy'), as said below
- charges: float32 [64, 16, 1024], P('gx', 'gy'), may hold values from -0.08 to 0.08
Outputs:
- potential: float32 [64, 16, 1024], P('gx', 'gy')
Inputs may be any that keep to these rules, and one draw needn't show every extreme that they name: `offsets`: particle p of a leaf lies in sub-cell (p // 4^2, (p // 4) % 4, p % 4) of the leaf's grid of 4^3 equal sub-cells, inside the middle half of that sub-cell along each dimension.
All inputs are finite; a program needn't handle non-finite values. Where the computation divides by a largest or mean magnitude, that divisor is 1e-20 or more.
Results may differ from a plain program's by a relative error of at most 0.0003.
Values sent between devices are 32-bit elements; how exact they have to be, the bound alone decides.
A program may use at most 192 MiB of HBM per device.

v0:
```python
import jax
import jax.numpy as jnp
from jax import lax
from jax.sharding import PartitionSpec as P

CX = 2
CY = 2
LZ = 16
PPL = 64
highest = lax.Precision.HIGHEST


def padded_2(block, sides, width):
    for axis, dim in sides:
        count = lax.axis_size(axis)
        forward = [(i, i + 1) for i in range(count - 1)]
        backward = [(target, source) for source, target in forward]
        low = lax.ppermute(
            lax.slice_in_dim(block, block.shape[dim] - width, None, axis=dim), axis, forward
        )
        high = lax.ppermute(lax.slice_in_dim(block, 0, width, axis=dim), axis, backward)
        block = jnp.concatenate([low, block, high], axis=dim)
    return block


def cheb_points():
    return jnp.cos((2.0 * jnp.arange(4, dtype=jnp.float32) + 1.0) * jnp.pi / 8.0)


def interpolate(coords):
    points = cheb_points()
    second = 2.0 * points * points - 1.0
    third = 4.0 * points * points * points - 3.0 * points
    value = coords[..., None]
    return 0.25 + 0.5 * (
        value * points
        + (2.0 * value * value - 1.0) * second
        + (4.0 * value * value * value - 3.0 * value) * third
    )


def node_grid():
    points = cheb_points()
    counter = jnp.arange(64, dtype=jnp.int32)
    return jnp.stack([points[counter // 16], points[counter // 4 % 4], points[counter % 4]], -1)


def child_grid():
    counter = jnp.arange(8, dtype=jnp.int32)
    return jnp.stack([counter // 4, counter // 2 % 2, counter % 2], -1).astype(jnp.float32)


def upward_matrix():
    points = cheb_points()
    halves = jnp.array([0.0, 1.0], dtype=jnp.float32)
    shifted = (points[None, :] + 2.0 * halves[:, None] - 1.0) / 2.0
    factor = interpolate(shifted)
    return jnp.einsum("xia,yjb,zkc->xyzijkabc", factor, factor, factor, precision=highest).reshape(
        512, 64
    )


def translation(offset):
    node_points = node_grid()
    child_corner = child_grid()
    box_offsets = 2.0 * offset[None, None, :] + child_corner[:, None, :] - child_corner[None, :, :]
    spread = (node_points[None, :, :] - node_points[:, None, :]) / 2.0
    separation = spread[None, :, None, :, :] - box_offsets[:, None, :, None, :]
    adjacent = (jnp.max(jnp.abs(box_offsets), -1) <= 1.0).astype(jnp.float32)[:, None, :, None]
    distance = jnp.sqrt(jnp.sum(separation * separation, -1))
    return ((1.0 - adjacent) / (distance + adjacent)).reshape(512, 512)


def offset_of(counter):
    return jnp.stack([counter // 9, counter // 3 % 3, counter % 3]) - 1


def translation_tables():

    def one_table(counter):
        return translation(offset_of(counter).astype(jnp.float32))

    return lax.map(one_table, jnp.arange(27, dtype=jnp.int32))


def to_parent(moments):
    size_x, size_y, size_z, _ = moments.shape
    moments = moments.reshape(size_x // 2, 2, size_y // 2, 2, size_z // 2, 2, 64)
    return moments.transpose(0, 2, 4, 1, 3, 5, 6).reshape(
        size_x // 2, size_y // 2, size_z // 2, 512
    )


def from_parent(moments):
    size_x, size_y, size_z, _ = moments.shape
    moments = moments.reshape(size_x, size_y, size_z, 2, 2, 2, 64)
    return moments.transpose(0, 3, 1, 4, 2, 5, 6).reshape(2 * size_x, 2 * size_y, 2 * size_z, 64)


def matmul(left, right):
    return jnp.dot(left, right, precision=highest, preferred_element_type=jnp.float32)


def coarsen(moments, upward):
    parents = to_parent(moments)
    return matmul(parents.reshape(-1, 512), upward).reshape(parents.shape[:3] + (64,))


def refine(local, upward):
    spread_out = matmul(local.reshape(-1, 64), upward.T).reshape(local.shape[:3] + (512,))
    return from_parent(spread_out)


def pad_one(moments):
    return jnp.pad(moments, ((1, 1), (1, 1), (1, 1), (0, 0)))


def far_translate(padded, scaling, tables):
    size_x, size_y, size_z = (padded.shape[0] - 2, padded.shape[1] - 2, padded.shape[2] - 2)

    def step_fn(running, inputs):
        counter, table = inputs
        offset = offset_of(counter)
        window_piece = lax.dynamic_slice(
            padded,
            (offset[0] + 1, offset[1] + 1, offset[2] + 1, jnp.int32(0)),
            (size_x, size_y, size_z, 512),
        )
        return (running + matmul(window_piece.reshape(-1, 512), table), None)

    running, _ = lax.scan(
        step_fn,
        jnp.zeros((size_x * size_y * size_z, 512), jnp.float32),
        (jnp.arange(27, dtype=jnp.int32), tables),
    )
    return (scaling * running).reshape(size_x, size_y, size_z, 512)


def dense_translate(targets, sources, weights):
    node_points = node_grid()
    spread = (node_points[:, None, :] - node_points[None, :, :]) / 2.0
    box_offsets = sources[None, :, :] - targets[:, None, :]
    separation = spread[None, :, None, :, :] - box_offsets[:, None, :, None, :]
    adjacent = (jnp.max(jnp.abs(box_offsets), -1) <= 1.0).astype(jnp.float32)[:, None, :, None]
    distance = jnp.sqrt(jnp.sum(separation * separation, -1))
    kernel = ((1.0 - adjacent) / (distance + adjacent)).reshape(
        targets.shape[0] * 64, sources.shape[0] * 64
    )
    return (0.125 * matmul(kernel, weights.reshape(-1))).reshape(targets.shape[0], 64)


def particle_basis(offsets):
    coords = 2.0 * offsets - 1.0
    along_x = interpolate(coords[0])
    along_y = interpolate(coords[1])
    along_z = interpolate(coords[2])
    product = (
        along_x[..., :, None, None] * along_y[..., None, :, None] * along_z[..., None, None, :]
    )
    return product.reshape(along_x.shape[:-1] + (64,))


def gather_moments(charges, interp_basis):
    return jnp.einsum(
        "...p,...pm->...m",
        charges,
        interp_basis,
        precision=highest,
        preferred_element_type=jnp.float32,
    )


def evaluate_local(interp_basis, local):
    return jnp.einsum(
        "...pm,...m->...p",
        interp_basis,
        local,
        precision=highest,
        preferred_element_type=jnp.float32,
    )


def near_field(targets, sources, weights):
    size_x, size_y, depth, count = (
        targets.shape[1],
        targets.shape[2],
        targets.shape[3],
        targets.shape[4],
    )
    self_mask = jnp.concatenate(
        [
            jnp.zeros((count, count), jnp.float32),
            jnp.eye(count, dtype=jnp.float32),
            jnp.zeros((count, count), jnp.float32),
        ],
        1,
    )
    running = jnp.zeros((size_x, size_y, depth, count), jnp.float32)
    for step_x in range(3):
        for step_y in range(3):
            window = sources[:, step_x : step_x + size_x, step_y : step_y + size_y]
            stacked = jnp.concatenate(
                [
                    window[..., 0:depth, :],
                    window[..., 1 : depth + 1, :],
                    window[..., 2 : depth + 2, :],
                ],
                -1,
            )
            charge_win = weights[step_x : step_x + size_x, step_y : step_y + size_y]
            charge_win = jnp.concatenate(
                [
                    charge_win[..., 0:depth, :],
                    charge_win[..., 1 : depth + 1, :],
                    charge_win[..., 2 : depth + 2, :],
                ],
                -1,
            )
            squared = jnp.zeros((size_x, size_y, depth, count, 3 * count), jnp.float32)
            for comp in range(3):
                differ = targets[comp][..., :, None] - stacked[comp][..., None, :]
                squared = squared + differ * differ
            if step_x == 1 and step_y == 1:
                inverse = lax.rsqrt(squared + self_mask) * (1.0 - self_mask)
            else:
                inverse = lax.rsqrt(squared)
            running = running + jnp.sum(inverse * charge_win[..., None, :], -1)
    return running


def body(offsets, charges):
    index_x = lax.axis_index("gx")
    index_y = lax.axis_index("gy")
    count_x = lax.axis_size("gx")
    count_y = lax.axis_size("gy")
    upward = upward_matrix()
    tables = translation_tables()
    stacked = jnp.concatenate([offsets, charges[None]], 0)
    own_basis = particle_basis(offsets.reshape(3, CX, CY, LZ, PPL))
    own_charges = charges.reshape(CX, CY, LZ, PPL)
    leaf_moments = gather_moments(own_charges, own_basis)
    rim_flat = padded_2(leaf_moments.reshape(CX, CY, LZ * 64), (("gx", 0), ("gy", 1)), 2)
    rim_moments = rim_flat.reshape(CX + 4, CY + 4, LZ, 64)
    near_block = padded_2(stacked, (("gx", 1), ("gy", 2)), 1).reshape(4, CX + 2, CY + 2, LZ, PPL)
    rim_padded = jnp.pad(rim_moments, ((0, 0), (0, 0), (2, 2), (0, 0)))
    leaf_far = from_parent(far_translate(to_parent(rim_padded), 1.0, tables))
    first_moments = coarsen(leaf_moments, upward)
    first_piece = first_moments.reshape(1, CY // 2, LZ // 2 * 64)
    gathered = lax.all_gather(first_piece, ("gx", "gy"), axis=0, tiled=True)
    first_whole = gathered.reshape(count_x, count_y * (CY // 2), LZ // 2, 64)
    second_whole = coarsen(first_whole, upward)
    first_block = lax.dynamic_slice(
        pad_one(to_parent(first_whole)),
        (index_x // 2, index_y // 2, 0, 0),
        (3, 3, LZ // 4 + 2, 512),
    )
    third_whole = coarsen(second_whole, upward)
    first_far = from_parent(far_translate(first_block, 0.5, tables))
    first_far = lax.dynamic_slice(first_far, (index_x % 2, index_y % 2, 0, 0), (1, 1, LZ // 2, 64))
    second_block = lax.dynamic_slice(
        pad_one(to_parent(second_whole)),
        (index_x // 4, index_y // 4, 0, 0),
        (3, 3, LZ // 8 + 2, 512),
    )
    second_far = from_parent(far_translate(second_block, 0.25, tables))
    second_far = lax.dynamic_slice(
        second_far, (index_x // 2 % 2, index_y // 2 % 2, 0, 0), (1, 1, LZ // 4, 64)
    )
    boxes_x, boxes_y, boxes_z = (count_x * CX // 8, count_y * CY // 8, LZ // 8)
    counter = jnp.arange(boxes_x * boxes_y * boxes_z, dtype=jnp.int32)
    sources = jnp.stack(
        [counter // (boxes_y * boxes_z), counter // boxes_z % boxes_y, counter % boxes_z], -1
    ).astype(jnp.float32)
    targets = jnp.stack(
        [
            jnp.full((boxes_z,), index_x // 4, jnp.int32),
            jnp.full((boxes_z,), index_y // 4, jnp.int32),
            jnp.arange(boxes_z, dtype=jnp.int32),
        ],
        -1,
    ).astype(jnp.float32)
    top_far = dense_translate(targets, sources, third_whole.reshape(-1, 64))
    second_local = refine(top_far.reshape(1, 1, boxes_z, 64), upward)
    second_local = (
        lax.dynamic_slice(
            second_local, (index_x // 2 % 2, index_y // 2 % 2, 0, 0), (1, 1, LZ // 4, 64)
        )
        + second_far
    )
    first_local = refine(second_local, upward)
    first_local = (
        lax.dynamic_slice(first_local, (index_x % 2, index_y % 2, 0, 0), (1, 1, LZ // 2, 64))
        + first_far
    )
    leaf_local = refine(first_local, upward) + leaf_far
    far_potential = evaluate_local(own_basis, leaf_local)
    padded = jnp.pad(near_block, ((0, 0), (0, 0), (0, 0), (1, 1), (0, 0)))
    grid_x = (index_x * CX - 1 + jnp.arange(CX + 2, dtype=jnp.int32)).astype(jnp.float32)
    grid_y = (index_y * CY - 1 + jnp.arange(CY + 2, dtype=jnp.int32)).astype(jnp.float32)
    grid_z = jnp.arange(-1, LZ + 1, dtype=jnp.int32).astype(jnp.float32)
    positions = jnp.stack(
        [
            padded[0] + grid_x[:, None, None, None],
            padded[1] + grid_y[None, :, None, None],
            padded[2] + grid_z[None, None, :, None],
        ]
    )
    near_potential = near_field(positions[:, 1:-1, 1:-1, 1:-1], positions, padded[3])
    return (far_potential + near_potential).reshape(CX, CY, LZ * PPL)


def solution(mesh):
    in_specs = (P(None, "gx", "gy", None), P("gx", "gy", None))
    out_specs = P("gx", "gy", None)
    return jax.shard_map(body, mesh=mesh, in_specs=in_specs, out_specs=out_specs, check_vma=False)
```

profile of v0, /device:TPU:1, one launch (start us, length us, event | category | flops | bytes accessed | tf_op | source)
XLA Modules:
  0.0 1349.1 jit_solution(7207719074054783453)
XLA Ops:
  9.9 5.6 collective-permute-start
  16.2 3.6 collective-permute-start.4
  22.0 2.4 compare_select_fusion.29
  24.4 2.4 compare_select_fusion.23
  27.7 2.6 multiply_bitcast_fusion
  30.2 6.6 dot_general.84
  36.9 6.0 reshape.1491
  43.3 75.7 %all_gather.3 = f32[256,1,512]{2,1,0:T(1,128)S(1)} all-gather(f32[1,1,512]{2,1,0:T(1,128)S(1)} %reshape_reshape.29), channel_id=1, replica_groups=mesh['gx'=32,'gy'=8] {'gx','gy'}, dimensions={0}, use_global_device_ids=true | all-gather | bytes 526336 | tf_op jit(solution)/shard_map/all_gather | solution.py:249
  129.6 2.9 reshape.1306
  137.7 354.1 %while.55 = (s32[]{:T(128)}, f32[27,512,512]{2,1,0:T(8,128)}, s32[27]{0:T(128)S(1)}, s32[]{:T(128)}, s32[1]{0:T(128)}, /*index=5*/s32[]{:T(128)}, s32[]{:T(128)}...) while((s32[]{:T(128)}, f32[27,512,512]{2,1,0:T(8,128)}, s32[27]{0:T(128)S(1)}, s32[]{:T(128)}, ...), condition=%wide.region_5.6_spmd, body=%wide.region_2.5_spmd.sunk | while | flops 2651413 | bytes 7449731 | solution.py:83
  144.9 2.3 compare_select_fusion.34
  171.1 2.3 compare_select_fusion.34
  184.2 2.3 compare_select_fusion.34
  197.2 2.3 compare_select_fusion.34
  210.3 2.3 compare_select_fusion.34
  492.7 263.9 %while.57 = (s32[]{:T(128)}, f32[4,512]{1,0:T(4,128)S(1)}, s32[27]{0:T(128)S(1)}, f32[3,3,6,512]{3,0,2,1:T(4,128)S(1)}, f32[27,512,512]{2,1,0:T(8,128)}, /*index...) while((s32[]{:T(128)}, f32[4,512]{1,0:T(4,128)S(1)}, ...), condition=%wide.region_9.10_spmd.clone, body=%wide.region_8.9_spmd.clone.sunk | while | flops 12587056 | bytes 1090143 | solution.py:131
  756.7 263.8 %while.56 = (s32[]{:T(128)}, f32[2,512]{1,0:T(2,128)S(1)}, s32[27]{0:T(128)S(1)}, f32[3,3,4,512]{3,0,2,1:T(4,128)S(1)}, f32[27,512,512]{2,1,0:T(8,128)}, /*index...) while((s32[]{:T(128)}, f32[2,512]{1,0:T(2,128)S(1)}, ...), condition=%wide.region_7.8_spmd.clone, body=%wide.region_6.7_spmd.clone.sunk | while | flops 6293552 | bytes 1069663 | solution.py:131
  1027.7 3.5 collective-permute-start.2
  1034.7 3.0 collective-permute-start.7
  1038.7 280.9 %while.58 = (s32[]{:T(128)}, f32[8,512]{1,0:T(8,128)S(1)}, s32[27]{0:T(128)S(1)}, f32[3,3,10,512]{3,2,1,0:T(8,128)S(1)}, f32[27,512,512]{2,1,0:T(8,128)}, /*inde...) while((s32[]{:T(128)}, f32[8,512]{1,0:T(8,128)S(1)}, ...), condition=%wide.region_11.12_spmd.clone, body=%wide.region_10.11_spmd.clone.sunk | while | flops 25174064 | bytes 1098335 | solution.py:131
  1321.1 3.3 fusion.63
  1328.0 4.6 multiply_reduce_fusion.3
  1332.6 7.4 multiply_reduce_fusion.10
  1340.0 8.3 multiply_reduce_fusion.9
  (1097 shorter events, 556.4 us)
Async XLA Ops:
  2.3 13.2 copy-start.3
  2.3 13.2 copy-start.4
  6.0 30.9 %copy-start = (f32[2,2,16,64,64]{4,3,2,1,0:T(8,128)}, f32[2,2,16,64,64]{4,3,2,1,0:T(8,128)S(1)}, u32[]{:S(2)}) copy-start(f32[2,2,16,64,64]{4,3,2,1,0:T(8,128)S(1)} %copy.105) | copy-start | bytes 3145732
  8.6 1016.3 %collective-permute-start.1 = (f32[2,2,1024]{2,1,0:T(2,128)}, f32[2,2,1024]{2,1,0:T(2,128)}, u32[]{:S(2)}, u32[]{:S(2)}) collective-permute-start(f32[2,2,1024]{2,1,0:T(2,128)} %reshape.1309), channel_id=1, source_target_pairs={{8,0},{16,8},{24,16},{32,24},{40,32},{48,40},{56,48},{64,56},{72,6... | collective-permute-start | bytes 49160 | tf_op jit(solution)/shard_map/ppermute | solution.py:21
  9.9 1013.5 %collective-permute-start = (f32[2,2,1024]{2,1,0:T(2,128)}, f32[2,2,1024]{2,1,0:T(2,128)}, u32[]{:S(2)}, u32[]{:S(2)}) collective-permute-start(f32[2,2,1024]{2,1,0:T(2,128)} %reshape.1309), channel_id=1, source_target_pairs={{0,8},{8,16},{16,24},{24,32},{32,40},{40,48},{48,56},{56,64},{64,7... | collective-permute-start | bytes 49160 | tf_op jit(solution)/shard_map/ppermute | solution.py:18
  16.2 1015.0 %collective-permute-start.4 = (f32[4,1,2,1024]{3,2,1,0:T(2,128)}, f32[4,1,2,1024]{3,2,1,0:T(2,128)}, u32[]{:S(2)}, u32[]{:S(2)}) collective-permute-start(f32[4,1,2,1024]{3,2,1,0:T(2,128)} %get-tuple-element.678), channel_id=1, source_target_pairs={{0,8},{8,16},{16,24},{24,32},{32,40},{40,48},{48,56},{56,64},{64,7... | collective-permute-start | bytes 98312 | tf_op jit(solution)/shard_map/ppermute | solution.py:18
  19.7 1011.5 %collective-permute-start.5 = (f32[4,1,2,1024]{3,2,1,0:T(2,128)}, f32[4,1,2,1024]{3,2,1,0:T(2,128)}, u32[]{:S(2)}, u32[]{:S(2)}) collective-permute-start(f32[4,1,2,1024]{3,2,1,0:T(2,128)} %get-tuple-element.679), channel_id=1, source_target_pairs={{8,0},{16,8},{24,16},{32,24},{40,32},{48,40},{56,48},{64,56},{72,6... | collective-permute-start | bytes 98312 | tf_op jit(solution)/shard_map/ppermute | solution.py:21
  756.7 264.0 %copy-start.5 = (f32[64,64]{1,0:T(8,128)S(1)}, f32[64,64]{1,0:T(8,128)}, u32[]{:S(2)}) copy-start(f32[64,64]{1,0:T(8,128)} %fusion.31) | copy-start | bytes 49156
  756.7 264.7 %copy-start.2 = (f32[2,2,2,64,64]{4,3,2,1,0:T(8,128)S(1)}, f32[2,2,2,64,64]{4,3,2,1,0:T(8,128)}, u32[]{:S(2)}) copy-start(f32[2,2,2,64,64]{4,3,2,1,0:T(8,128)} %dot_general.84) | copy-start | bytes 393220
  1025.6 12.1 collective-permute-start.3
  1027.7 10.1 collective-permute-start.2
  1032.8 291.7 %collective-permute-start.6 = (f32[4,4,1,1024]{3,2,1,0:T(1,128)}, f32[4,4,1,1024]{3,2,1,0:T(1,128)}, u32[]{:S(2)}, u32[]{:S(2)}) collective-permute-start(f32[4,4,1,1024]{3,2,1,0:T(1,128)} %get-tuple-element.674), channel_id=1, source_target_pairs={{0,1},{1,2},{2,3},{3,4},{4,5},{5,6},{6,7},{8,9},{9,10},{10,11},{11... | collective-permute-start | bytes 196616 | tf_op jit(solution)/shard_map/ppermute | solution.py:18
  1034.7 289.8 %collective-permute-start.7 = (f32[4,4,1,1024]{3,2,1,0:T(1,128)}, f32[4,4,1,1024]{3,2,1,0:T(1,128)}, u32[]{:S(2)}, u32[]{:S(2)}) collective-permute-start(f32[4,4,1,1024]{3,2,1,0:T(1,128)} %get-tuple-element.675), channel_id=1, source_target_pairs={{1,0},{2,1},{3,2},{4,3},{5,4},{6,5},{7,6},{9,8},{10,9},{11,10},{12... | collective-permute-start | bytes 196616 | tf_op jit(solution)/shard_map/ppermute | solution.py:21
  1038.2 282.9 %copy-start.1 = (f32[2,2,16,64,64]{4,3,2,1,0:T(8,128)S(1)}, f32[2,2,16,64,64]{4,3,2,1,0:T(8,128)}, u32[]{:S(2)}) copy-start(f32[2,2,16,64,64]{4,3,2,1,0:T(8,128)} %copy-done) | copy-start | bytes 3145732
  1038.7 287.2 %copy-start.8 = (f32[4]{0:T(128)S(1)}, f32[4]{0:T(128)}, u32[]{:S(2)}) copy-start(f32[4]{0:T(128)} %add_convert_fusion.5) | copy-start | bytes 52
  1327.0 5.7 copy-start.6
  1327.0 5.7 copy-start.7
where the time goes:
time: 1360 us; the launch traced here: 1350 us
  loops' own time  642 us (47%)
  other arithmetic  235 us (17%)
  local copies, waits for them, and re-layouts  212 us (16%)
  matrix products  161 us (12%)
  blocking collectives  75.7 us (6%)
  starting transfers between devices  22.2 us (2%)
    another operation x3, loops' own time, far_translate(): lax.scan(step_fn, jnp.zeros((size_x * size_y * size_z, 512), jnp.float32)...  554 us
    dot_general x88, matrix products, matmul(): jnp.dot(left, right, precision=highest, preferred_element_type=jnp.float32)  155 us
    another operation x1, loops' own time, translation_tables(): return lax.map(one_table, jnp.arange(27, dtype=jnp.int32))  88.1 us
    all_gather x1, blocking collectives, body(): gathered = lax.all_gather(first_piece, ('gx', 'gy'), axis=0, tiled=True)  75.7 us
    gather x28, other arithmetic, node_grid(): points[counter % 4]  65.8 us
    gather x28, other arithmetic, node_grid(): points[counter // 16]  65.6 us
    dynamic_slice x108, local copies, waits for them, and re-layouts, translation_tables(): return lax.map(one_table, jnp.arange(27, dtype=jnp.int32))  63.8 us
    slice x81, local copies, waits for them, and re-layouts, step_fn(): offset[2] + 1  50.2 us
  transfers between devices with their start and end apart: 8, of which 0 were waited for; matrix products, arithmetic and copies ran while one was open for 43% of the time, Pallas kernels for 0%

commit v1 on v0

--- a/solution.py
+++ b/solution.py
@@ -246,7 +246,8 @@
     leaf_far = from_parent(far_translate(to_parent(rim_padded), 1.0, tables))
     first_moments = coarsen(leaf_moments, upward)
     first_piece = first_moments.reshape(1, CY // 2, LZ // 2 * 64)
-    gathered = lax.all_gather(first_piece, ("gx", "gy"), axis=0, tiled=True)
+    outgoing = jnp.stack([first_piece] * lax.axis_size(("gx", "gy")))
+    gathered = jnp.concatenate(lax.all_to_all(outgoing, ("gx", "gy"), 0, 0), axis=0)
     first_whole = gathered.reshape(count_x, count_y * (CY // 2), LZ // 2, 64)
     second_whole = coarsen(first_whole, upward)
     first_block = lax.dynamic_slice(

time: 1360 us -> 1330 us (0.978)
  blocking collectives: 75.7 us -> 0 us
  starting transfers between devices: 22.2 us -> 40.3 us
    all_gather x1 -> x0, blocking collectives: 75.7 us -> none  [body(): gathered = lax.all_gather(first_piece, ('gx', 'gy'), axis=0, tiled=True)]
    all_to_all x0 -> x1, starting transfers between devices: none -> 17.8 us  [body(): lax.all_to_all(outgoing, ('gx', 'gy'), 0, 0)]
  transfers between devices with their start and end apart: 8 -> 9, of which waited for: 0 -> 0; matrix products, arithmetic and copies ran while one was open for 43% -> 32% of each run, Pallas kernels for 0% -> 0%
where the time goes in v1:
time: 1330 us; the launch traced here: 1310 us
  loops' own time  655 us (49%)
  other arithmetic  248 us (19%)
  local copies, waits for them, and re-layouts  211 us (16%)
  matrix products  159 us (12%)
  starting transfers between devices  40.3 us (3%)
    another operation x3, loops' own time, far_translate(): lax.scan(step_fn, jnp.zeros((size_x * size_y * size_z, 512), jnp.float32)...  567 us
    dot_general x88, matrix products, matmul(): jnp.dot(left, right, precision=highest, preferred_element_type=jnp.float32)  154 us
    another operation x1, loops' own time, translation_tables(): return lax.map(one_table, jnp.arange(27, dtype=jnp.int32))  87.6 us
    gather x28, other arithmetic, node_grid(): points[counter % 4]  69 us
    gather x28, other arithmetic, node_grid(): points[counter // 16]  68.8 us
    dynamic_slice x108, local copies, waits for them, and re-layouts, translation_tables(): return lax.map(one_table, jnp.arange(27, dtype=jnp.int32))  64.9 us
    slice x81, local copies, waits for them, and re-layouts, step_fn(): offset[2] + 1  50.6 us
    reduce_sum x27, other arithmetic, translation(): distance = jnp.sqrt(jnp.sum(separation * separation, -1))  30.7 us
  transfers between devices with their start and end apart: 9, of which 0 were waited for; matrix products, arithmetic and copies ran while one was open for 32% of the time, Pallas kernels for 0%

profile of v1, /device:TPU:1, one launch (start us, length us, event | category | flops | bytes accessed | tf_op | source)
XLA Modules:
  0.0 1313.5 jit_solution(11579519985651891439)
XLA Ops:
  9.3 5.6 collective-permute-start
  15.6 3.6 collective-permute-start.4
  20.8 2.6 multiply_bitcast_fusion
  23.4 6.0 reshape.1495
  30.8 17.8 %all-to-all-start = ((f32[256,1,1,512]{3,2,1,0:T(1,128)}), f32[256,1,1,512]{3,2,1,0:T(1,128)}, u32[]{:S(2)}, u32[]{:S(2)}) async-start(f32[256,1,1,512]{3,2,1,0:T(1,128)} %stack.167), calls=%async_computation | async-start | bytes 1048576 | tf_op jit(solution)/shard_map/all_to_all | solution.py:250
  50.7 2.5 compare_select_fusion.29
  53.2 2.5 compare_select_fusion.23
  57.2 361.4 %while.55 = (s32[]{:T(128)}, f32[27,512,512]{2,1,0:T(8,128)}, s32[27]{0:T(128)S(1)}, s32[]{:T(128)}, s32[1]{0:T(128)}, /*index=5*/s32[]{:T(128)}, s32[]{:T(128)}...) while((s32[]{:T(128)}, f32[27,512,512]{2,1,0:T(8,128)}, s32[27]{0:T(128)S(1)}, s32[]{:T(128)}, ...), condition=%wide.region_5.6_spmd, body=%wide.region_2.5_spmd.sunk | while | flops 2651413 | bytes 7450651 | solution.py:83
  64.3 2.5 compare_select_fusion.34
  77.7 2.5 compare_select_fusion.34
  91.1 2.5 compare_select_fusion.34
  104.4 2.5 compare_select_fusion.34
  117.8 2.5 compare_select_fusion.34
  131.2 2.5 compare_select_fusion.34
  423.2 6.6 dot_general.84
  431.9 4.3 collective-permute-start.3
  441.1 2.6 collective-permute-start.7
  444.7 280.0 %while.58 = (s32[]{:T(128)}, f32[8,512]{1,0:T(8,128)S(1)}, s32[27]{0:T(128)S(1)}, f32[3,3,10,512]{3,2,1,0:T(8,128)S(1)}, f32[27,512,512]{2,1,0:T(8,128)}, /*inde...) while((s32[]{:T(128)}, f32[8,512]{1,0:T(8,128)S(1)}, ...), condition=%wide.region_11.12_spmd.clone, body=%wide.region_10.11_spmd.clone.sunk | while | flops 25174064 | bytes 1098335 | solution.py:131
  728.1 5.1 multiply_reduce_fusion.3
  733.2 8.8 multiply_reduce_fusion.9
  742.1 8.3 multiply_reduce_fusion.10
  764.4 271.6 %while.57 = (s32[]{:T(128)}, f32[4,512]{1,0:T(4,128)S(1)}, s32[27]{0:T(128)S(1)}, f32[3,3,6,512]{3,0,2,1:T(4,128)S(1)}, f32[27,512,512]{2,1,0:T(8,128)}, /*index...) while((s32[]{:T(128)}, f32[4,512]{1,0:T(4,128)S(1)}, ...), condition=%wide.region_9.10_spmd.clone, body=%wide.region_8.9_spmd.clone.sunk | while | flops 12587056 | bytes 1090143 | solution.py:131
  1036.1 271.5 %while.56 = (s32[]{:T(128)}, f32[2,512]{1,0:T(2,128)S(1)}, s32[27]{0:T(128)S(1)}, f32[3,3,4,512]{3,0,2,1:T(4,128)S(1)}, f32[27,512,512]{2,1,0:T(8,128)}, /*index...) while((s32[]{:T(128)}, f32[2,512]{1,0:T(2,128)S(1)}, ...), condition=%wide.region_7.8_spmd.clone, body=%wide.region_6.7_spmd.clone.sunk | while | flops 6293552 | bytes 1069663 | solution.py:131
  1309.4 3.3 fusion.63
  (1225 shorter events, 563.5 us)
Async XLA Ops:
  6.0 23.4 %copy-start = (f32[2,2,16,64,64]{4,3,2,1,0:T(8,128)}, f32[2,2,16,64,64]{4,3,2,1,0:T(8,128)S(1)}, u32[]{:S(2)}) copy-start(f32[2,2,16,64,64]{4,3,2,1,0:T(8,128)S(1)} %copy.88) | copy-start | bytes 3145732
  8.0 423.2 %collective-permute-start.1 = (f32[2,2,1024]{2,1,0:T(2,128)S(1)}, f32[2,2,1024]{2,1,0:T(2,128)}, u32[]{:S(2)}, u32[]{:S(2)}) collective-permute-start(f32[2,2,1024]{2,1,0:T(2,128)S(1)} %reshape.1313), channel_id=1, source_target_pairs={{8,0},{16,8},{24,16},{32,24},{40,32},{48,40},{56,48},{64,56},{72,6... | collective-permute-start | bytes 49160 | tf_op jit(solution)/shard_map/ppermute | solution.py:21
  9.3 421.1 %collective-permute-start = (f32[2,2,1024]{2,1,0:T(2,128)S(1)}, f32[2,2,1024]{2,1,0:T(2,128)}, u32[]{:S(2)}, u32[]{:S(2)}) collective-permute-start(f32[2,2,1024]{2,1,0:T(2,128)S(1)} %reshape.1313), channel_id=1, source_target_pairs={{0,8},{8,16},{16,24},{24,32},{32,40},{40,48},{48,56},{56,64},{64,7... | collective-permute-start | bytes 49160 | tf_op jit(solution)/shard_map/ppermute | solution.py:18
  15.6 422.6 %collective-permute-start.4 = (f32[4,1,2,1024]{3,2,1,0:T(2,128)}, f32[4,1,2,1024]{3,2,1,0:T(2,128)}, u32[]{:S(2)}, u32[]{:S(2)}) collective-permute-start(f32[4,1,2,1024]{3,2,1,0:T(2,128)} %get-tuple-element.668), channel_id=1, source_target_pairs={{0,8},{8,16},{16,24},{24,32},{32,40},{40,48},{48,56},{56,64},{64,7... | collective-permute-start | bytes 98312 | tf_op jit(solution)/shard_map/ppermute | solution.py:18
  19.2 419.0 %collective-permute-start.5 = (f32[4,1,2,1024]{3,2,1,0:T(2,128)}, f32[4,1,2,1024]{3,2,1,0:T(2,128)}, u32[]{:S(2)}, u32[]{:S(2)}) collective-permute-start(f32[4,1,2,1024]{3,2,1,0:T(2,128)} %get-tuple-element.669), channel_id=1, source_target_pairs={{8,0},{16,8},{24,16},{32,24},{40,32},{48,40},{56,48},{64,56},{72,6... | collective-permute-start | bytes 98312 | tf_op jit(solution)/shard_map/ppermute | solution.py:21
  30.8 719.6 %all-to-all-start = ((f32[256,1,1,512]{3,2,1,0:T(1,128)}), f32[256,1,1,512]{3,2,1,0:T(1,128)}, u32[]{:S(2)}, u32[]{:S(2)}) async-start(f32[256,1,1,512]{3,2,1,0:T(1,128)} %stack.167), calls=%async_computation | async-start | bytes 1048576 | tf_op jit(solution)/shard_map/all_to_all | solution.py:250
  431.9 11.8 collective-permute-start.3
  436.2 7.5 collective-permute-start.2
  439.1 285.7 %collective-permute-start.6 = (f32[4,4,1,1024]{3,2,1,0:T(1,128)S(1)}, f32[4,4,1,1024]{3,2,1,0:T(1,128)S(1)}, u32[]{:S(2)}, u32[]{:S(2)}) collective-permute-start(f32[4,4,1,1024]{3,2,1,0:T(1,128)S(1)} %get-tuple-element.664), channel_id=1, source_target_pairs={{0,1},{1,2},{2,3},{3,4},{4,5},{5,6},{6,7},{8,9},{9,10},{10,11},{11... | collective-permute-start | bytes 196616 | tf_op jit(solution)/shard_map/ppermute | solution.py:18
  441.1 283.7 %collective-permute-start.7 = (f32[4,4,1,1024]{3,2,1,0:T(1,128)S(1)}, f32[4,4,1,1024]{3,2,1,0:T(1,128)S(1)}, u32[]{:S(2)}, u32[]{:S(2)}) collective-permute-start(f32[4,4,1,1024]{3,2,1,0:T(1,128)S(1)} %get-tuple-element.665), channel_id=1, source_target_pairs={{1,0},{2,1},{3,2},{4,3},{5,4},{6,5},{7,6},{9,8},{10,9},{11,10},{12... | collective-permute-start | bytes 196616 | tf_op jit(solution)/shard_map/ppermute | solution.py:21
  444.3 281.7 %copy-start.16 = (f32[18]{0:T(128)S(1)}, f32[18]{0:T(128)}, u32[]{:S(2)}) copy-start(f32[18]{0:T(128)} %add_convert_fusion.3) | copy-start | bytes 220
  444.3 281.7 %copy-start.17 = (f32[4]{0:T(128)S(1)}, f32[4]{0:T(128)}, u32[]{:S(2)}) copy-start(f32[4]{0:T(128)} %add_convert_fusion.5) | copy-start | bytes 52
  728.1 14.0 %copy-start.6 = (f32[64,192]{1,0:T(8,128)S(1)}, f32[64,192]{1,0:T(8,128)}, u32[]{:S(2)}) copy-start(f32[64,192]{1,0:T(8,128)} %get-tuple-element.666) | copy-start | bytes 147460
  728.1 14.0 %copy-start.7 = (f32[64,192]{1,0:T(8,128)S(1)}, f32[64,192]{1,0:T(8,128)}, u32[]{:S(2)}) copy-start(f32[64,192]{1,0:T(8,128)} %get-tuple-element.667) | copy-start | bytes 147460
  764.3 543.4 %copy-start.3 = (f32[2,2,2,64,64]{4,3,2,1,0:T(8,128)S(1)}, f32[2,2,2,64,64]{4,3,2,1,0:T(8,128)}, u32[]{:S(2)}) copy-start(f32[2,2,2,64,64]{4,3,2,1,0:T(8,128)} %dot_general.84) | copy-start | bytes 393220
  1036.0 273.4 %copy-start.1 = (f32[2,2,16,64,64]{4,3,2,1,0:T(8,128)S(1)}, f32[2,2,16,64,64]{4,3,2,1,0:T(8,128)}, u32[]{:S(2)}) copy-start(f32[2,2,16,64,64]{4,3,2,1,0:T(8,128)} %copy-done) | copy-start | bytes 3145732
  1036.0 276.7 %copy-start.8 = (f32[2,2,16,64]{3,2,1,0:T(8,128)S(1)}, f32[2,2,16,64]{3,2,1,0:T(8,128)}, u32[]{:S(2)}) copy-start(f32[2,2,16,64]{3,2,1,0:T(8,128)} %get-tuple-element.521) | copy-start | bytes 49156
  1036.1 276.7 %copy-start.9 = (f32[2,2,16,64]{3,2,1,0:T(8,128)S(1)}, f32[2,2,16,64]{3,2,1,0:T(8,128)}, u32[]{:S(2)}) copy-start(f32[2,2,16,64]{3,2,1,0:T(8,128)} %get-tuple-element.513) | copy-start | bytes 49156
  1036.1 276.7 %copy-start.10 = (f32[2,2,16,64]{3,2,1,0:T(8,128)S(1)}, f32[2,2,16,64]{3,2,1,0:T(8,128)}, u32[]{:S(2)}) copy-start(f32[2,2,16,64]{3,2,1,0:T(8,128)} %get-tuple-element.514) | copy-start | bytes 49156
  1036.1 276.7 %copy-start.11 = (f32[2,2,16,64]{3,2,1,0:T(8,128)S(1)}, f32[2,2,16,64]{3,2,1,0:T(8,128)}, u32[]{:S(2)}) copy-start(f32[2,2,16,64]{3,2,1,0:T(8,128)} %get-tuple-element.515) | copy-start | bytes 49156
  1036.1 276.7 %copy-start.12 = (f32[2,2,16,64]{3,2,1,0:T(8,128)S(1)}, f32[2,2,16,64]{3,2,1,0:T(8,128)}, u32[]{:S(2)}) copy-start(f32[2,2,16,64]{3,2,1,0:T(8,128)} %get-tuple-element.516) | copy-start | bytes 49156
  1036.1 276.7 %copy-start.13 = (f32[2,2,16,64]{3,2,1,0:T(8,128)S(1)}, f32[2,2,16,64]{3,2,1,0:T(8,128)}, u32[]{:S(2)}) copy-start(f32[2,2,16,64]{3,2,1,0:T(8,128)} %get-tuple-element.517) | copy-start | bytes 49156
  1036.1 276.7 %copy-start.14 = (f32[2,2,16,64]{3,2,1,0:T(8,128)S(1)}, f32[2,2,16,64]{3,2,1,0:T(8,128)}, u32[]{:S(2)}) copy-start(f32[2,2,16,64]{3,2,1,0:T(8,128)} %get-tuple-element.518) | copy-start | bytes 49156
  1036.1 276.7 %copy-start.15 = (f32[2,2,16,64]{3,2,1,0:T(8,128)S(1)}, f32[2,2,16,64]{3,2,1,0:T(8,128)}, u32[]{:S(2)}) copy-start(f32[2,2,16,64]{3,2,1,0:T(8,128)} %get-tuple-element.519) | copy-start | bytes 49156
  (57 other events, 197.1 us)
